TPU v7x, 32 devices: a whole 2x2x4 slice. The times are simulated.
32 devices in a mesh: gx: 2 (over x), gy: 4 (over y, core), gz: 4 (over z).
Axes of the slice: x: 2, y: 2, z: 4, core: 2. Of those that a mesh axis runs over, the one named last changes fastest.
Arguments:
- solid_state: float32 [9, 32, 16, 512], P(None, 'gz', 'gx', 'gy'), may hold values from -6 to 6
- material: float32 [4, 32, 16, 512], P(None, 'gz', 'gx', 'gy'), may hold values from 0.5 to 2
- ocean_state: float32 [4, 16, 32, 1024], P(None, None, 'gx', ('gy', 'gz')), may hold values from -6 to 6
- ocean_medium: float32 [2, 16], replicated, may hold values from 0.5 to 2
- offset_x: int32 [32], P('gx'), may hold values from -1 to 1
- offset_y: int32 [1024], P(('gy', 'gz')), may hold values from -1 to 1
Outputs:
- solid_next: float32 [9, 32, 16, 512], P(None, 'gz', 'gx', 'gy')
- solid_rate: float32 [9, 32, 16, 512], P(None, 'gz', 'gx', 'gy')
- ocean_next: float32 [4, 16, 32, 1024], P(None, None, 'gx', ('gy', 'gz'))
- ocean_rate: float32 [4, 16, 32, 1024], P(None, None, 'gx', ('gy', 'gz'))
All inputs are finite; a program needn't handle non-finite values.
Results may differ from a plain program's by a relative error of at most 0.000059.
Values sent between devices are 32-bit elements; how exact they have to be, the bound alone decides.
No kernel may reach another device: no remote copies, remote signals or barrier semaphores. Data moves between devices by JAX's collectives and lax.ppermute only.
A program may use at most 64 MiB of HBM per device.

v0:
```python
import jax
import jax.numpy as jnp
from jax import lax
from jax.sharding import PartitionSpec as P

closure_rows = (
    (-24.0 / 17.0, 59.0 / 34.0, -4.0 / 17.0, -3.0 / 34.0, 0.0, 0.0),
    (-0.5, 0.0, 0.5, 0.0, 0.0, 0.0),
    (4.0 / 43.0, -59.0 / 86.0, 0.0, 59.0 / 86.0, -4.0 / 43.0, 0.0),
    (3.0 / 98.0, 0.0, -59.0 / 98.0, 0.0, 32.0 / 49.0, -4.0 / 49.0),
)
inv_norm = 48.0 / 17.0
step_size = 0.25
section_weight = 0.1496590219993
gravity = 0.4


def with_halo(x, sides, width):
    for axis, dim in sides:
        size, length = (lax.axis_size(axis), x.shape[dim])
        up = [(i, (i + 1) % size) for i in range(size - 1)]
        down = [(j, i) for i, j in up]
        last = lax.slice_in_dim(x, length - width, length, axis=dim)
        leading = lax.slice_in_dim(x, 0, width, axis=dim)
        before = lax.ppermute(last, axis, up)
        after = lax.ppermute(leading, axis, down)
        x = jnp.concatenate([before, x, after], axis=dim)
    return x


def broadcast(block, axis, owner):
    block = jnp.where(lax.axis_index(axis) == owner, block, jnp.zeros_like(block))
    return lax.psum(block, axis)


def take_slab(field, first_index, length, dimension):
    return lax.slice_in_dim(field, first_index, first_index + length, axis=dimension)


def closure(field, dimension, at_end):
    extent = field.shape[dimension]
    pieces = []
    for row_index in range(4):
        running = jnp.zeros_like(take_slab(field, 0, 1, dimension))
        for col_index in range(6):
            weight = closure_rows[row_index][col_index]
            if weight != 0.0:
                if at_end:
                    running = running - weight * take_slab(
                        field, extent - 1 - col_index, 1, dimension
                    )
                else:
                    running = running + weight * take_slab(field, col_index, 1, dimension)
        pieces.append(running)
    if at_end:
        pieces = pieces[::-1]
    return jnp.concatenate(pieces, axis=dimension)


def interior(padded, dimension, extent):
    return (
        take_slab(padded, 0, extent, dimension)
        - 8.0 * take_slab(padded, 1, extent, dimension)
        + 8.0 * take_slab(padded, 3, extent, dimension)
        - take_slab(padded, 4, extent, dimension)
    ) / 12.0


def derivative(field, dimension):
    extent = field.shape[dimension]
    widths = [(0, 0)] * field.ndim
    widths[dimension] = (2, 2)
    middle = interior(jnp.pad(field, widths), dimension, extent)
    return jnp.concatenate(
        [
            closure(field, dimension, False),
            take_slab(middle, 4, extent - 8, dimension),
            closure(field, dimension, True),
        ],
        axis=dimension,
    )


def local_derivative(padded, field, dimension, is_first, is_last):
    extent = field.shape[dimension]
    middle = interior(padded, dimension, extent)
    head = jnp.where(is_first, closure(field, dimension, False), take_slab(middle, 0, 4, dimension))
    tail = jnp.where(
        is_last, closure(field, dimension, True), take_slab(middle, extent - 4, 4, dimension)
    )
    return jnp.concatenate(
        [head, take_slab(middle, 4, extent - 8, dimension), tail], axis=dimension
    )


def blend_matrix(offsets, fine_first, coarse_first, columns, coarse_total):
    fine_index = fine_first + jnp.arange(offsets.shape[0], dtype=jnp.int32)
    coarse = fine_index // 2
    target = jnp.clip(coarse + offsets, 0, coarse_total - 1)
    column = jnp.arange(columns, dtype=jnp.int32)[None, :]
    nearest = (column == (coarse - coarse_first)[:, None]).astype(jnp.float32)
    farther = (column == (target - coarse_first)[:, None]).astype(jnp.float32)
    return 0.75 * nearest + 0.25 * farther


def restrict(bottom):
    fine_rows, fine_cols = bottom.shape
    return bottom.reshape(fine_rows // 2, 2, fine_cols // 2, 2).mean(axis=(1, 3))


def solid_rates(material, diff_x, diff_y, diff_z):
    buoyancy = material[0]
    lame_one = material[1]
    lame_two = material[2]
    metric = material[3]

    def vertical(member):
        return metric * diff_z(member)

    strain_xx = diff_x(0)
    strain_yy = diff_y(1)
    strain_zz = vertical(2)
    dilation = strain_xx + strain_yy + strain_zz
    return [
        buoyancy * (diff_x(3) + diff_y(8) + vertical(7)),
        buoyancy * (diff_x(8) + diff_y(4) + vertical(6)),
        buoyancy * (diff_x(7) + diff_y(6) + vertical(5)),
        lame_one * dilation + 2.0 * lame_two * strain_xx,
        lame_one * dilation + 2.0 * lame_two * strain_yy,
        lame_one * dilation + 2.0 * lame_two * strain_zz,
        lame_two * (vertical(1) + diff_y(2)),
        lame_two * (vertical(0) + diff_x(2)),
        lame_two * (diff_y(0) + diff_x(1)),
    ]


def seafloor_terms(state, material, bed_pressure):
    factor = inv_norm * material[0, 0] * material[3, 0]
    return (factor * state[7, 0], factor * state[6, 0], factor * (state[5, 0] + bed_pressure))


def ocean_rates(state, medium, diff_x, diff_y, bed_speed):
    bulk = medium[0][:, None, None]
    light = medium[1][:, None, None]
    pressure = state[0]
    flow_z = state[3]
    rate_p = (
        -bulk * (2.0 * diff_x(1) + 2.0 * diff_y(2) + derivative(flow_z, 0))
        + gravity * flow_z / light
    )
    rate_p = rate_p.at[-1].add(inv_norm * bulk[-1] * (flow_z[-1] - bed_speed))
    rate_u = -2.0 * light * diff_x(0)
    rate_v = -2.0 * light * diff_y(0)
    rate_w = -light * derivative(pressure, 0)
    rate_w = rate_w.at[0].add(-inv_norm * light[0] * pressure[0])
    return jnp.stack([rate_p, rate_u, rate_v, rate_w])


def body(solid_state, material, ocean_state, ocean_medium, offset_x, offset_y):
    highest = lax.Precision.HIGHEST
    span_x = lax.axis_size("gx")
    span_y = lax.axis_size("gy")
    span_z = lax.axis_size("gz")
    index_x = lax.axis_index("gx")
    index_y = lax.axis_index("gy")
    index_z = lax.axis_index("gz")
    cells_x = solid_state.shape[2]
    cells_y = solid_state.shape[3]
    column_width = ocean_state.shape[3]
    x_first = index_x == 0
    x_last = index_x == span_x - 1
    y_first = index_y == 0
    y_last = index_y == span_y - 1
    z_first = index_z == 0
    z_last = index_z == span_z - 1
    joint_first = jnp.logical_and(y_first, z_first)
    joint_last = jnp.logical_and(y_last, z_last)
    plane = solid_state[2, 0]
    rimmed = with_halo(plane, (("gx", 0), ("gy", 1)), 1)
    shared = broadcast(rimmed, "gz", 0)
    bottom_part = restrict(ocean_state[0, -1])
    bed_pressure = lax.all_gather(bottom_part, "gz", axis=1, tiled=True)
    ocean_rim = with_halo(ocean_state[0:3], (("gx", 2), (("gy", "gz"), 3)), 2)
    x_fields = (0, 1, 2, 3, 8, 7)
    y_fields = (0, 1, 2, 4, 8, 6)
    z_fields = (0, 1, 2, 5, 6, 7)
    sent_x = with_halo(jnp.stack([solid_state[member] for member in x_fields]), (("gx", 2),), 2)
    sent_y = with_halo(jnp.stack([solid_state[member] for member in y_fields]), (("gy", 3),), 2)
    sent_z = with_halo(jnp.stack([solid_state[member] for member in z_fields]), (("gz", 1),), 2)

    def padded_x(member):
        return sent_x[x_fields.index(member)]

    def padded_y(member):
        return sent_y[y_fields.index(member)]

    def padded_z(member):
        return sent_z[z_fields.index(member)]

    rates = solid_rates(
        material,
        lambda member: local_derivative(padded_x(member), solid_state[member], 1, x_first, x_last),
        lambda member: local_derivative(padded_y(member), solid_state[member], 2, y_first, y_last),
        lambda member: local_derivative(padded_z(member), solid_state[member], 0, z_first, z_last),
    )
    term_x, term_y, term_z = seafloor_terms(solid_state, material, bed_pressure)
    rates[0] = rates[0].at[0].add(jnp.where(z_first, term_x, 0.0))
    rates[1] = rates[1].at[0].add(jnp.where(z_first, term_y, 0.0))
    rates[2] = rates[2].at[0].add(jnp.where(z_first, term_z, 0.0))
    solid_rate = step_size * jnp.stack(rates)
    solid_next = solid_state + section_weight * solid_rate
    blend_x = blend_matrix(
        offset_x, index_x * 2 * cells_x, index_x * cells_x - 1, cells_x + 2, cells_x * span_x
    )
    blend_y = blend_matrix(
        offset_y,
        index_y * 2 * cells_y + index_z * column_width,
        index_y * cells_y - 1,
        cells_y + 2,
        cells_y * span_y,
    )
    bed_speed = jnp.dot(jnp.dot(blend_x, shared, precision=highest), blend_y.T, precision=highest)
    ocean_rate = step_size * ocean_rates(
        ocean_state,
        ocean_medium,
        lambda member: local_derivative(
            ocean_rim[member, :, :, 2:-2], ocean_state[member], 1, x_first, x_last
        ),
        lambda member: local_derivative(
            ocean_rim[member, :, 2:-2, :], ocean_state[member], 2, joint_first, joint_last
        ),
        bed_speed,
    )
    ocean_next = ocean_state + section_weight * ocean_rate
    return (solid_next, solid_rate, ocean_next, ocean_rate)


def solution(mesh):
    in_specs = (
        P(None, "gz", "gx", "gy"),
        P(None, "gz", "gx", "gy"),
        P(None, None, "gx", ("gy", "gz")),
        P(),
        P("gx"),
        P(("gy", "gz")),
    )
    out_specs = (
        P(None, "gz", "gx", "gy"),
        P(None, "gz", "gx", "gy"),
        P(None, None, "gx", ("gy", "gz")),
        P(None, None, "gx", ("gy", "gz")),
    )
    return jax.shard_map(body, mesh=mesh, in_specs=in_specs, out_specs=out_specs, check_vma=False)
```

profile of v0, /device:TPU:14, one launch (start us, length us, event | category | flops | bytes accessed | tf_op | source)
XLA Modules:
  0.0 214.7 jit_solution(6294805913132325502)
XLA Ops:
  0.6 1.7 fusion.201
  2.3 1.3 collective-permute-start.6
  3.6 5.8 %collective-permute-start.7 = (f32[3,16,2,64]{3,2,1,0:T(2,128)}, f32[3,16,2,64]{3,2,1,0:T(2,128)}, u32[]{:S(2)}, u32[]{:S(2)}) collective-permute-start(f32[3,16,2,64]{3,2,1,0:T(2,128)} %get-tuple-element.115), channel_id=1, source_target_pairs={{16,0},{17,1},{18,2},{19,3},{20,4},{21,5},{22,6},{23,7},{24,8},{25... | collective-permute-start | bytes 73736 | tf_op jit(solution)/shard_map/ppermute | solution.py:26
  9.4 1.3 slice_bitcast_fusion.42
  10.7 1.3 collective-permute-start.10
  12.0 5.8 %collective-permute-start.11 = (f32[1,128]{1,0:T(1,128)}, f32[1,128]{1,0:T(1,128)}, u32[]{:S(2)}, u32[]{:S(2)}) collective-permute-start(f32[1,128]{1,0:T(1,128)} %get-tuple-element.135), channel_id=1, source_target_pairs={{16,0},{17,1},{18,2},{19,3},{20,4},{21,5},{22,6},{23,7},{24,8},{25... | collective-permute-start | bytes 1544 | tf_op jit(solution)/shard_map/ppermute | solution.py:26
  17.8 1.5 slice_bitcast_fusion.23
  20.7 1.3 collective-permute-start
  22.0 1.7 slice_multiply_fusion.35
  26.6 0.8 multiply_add_fusion.14
  31.9 0.9 multiply_add_fusion.2
  39.5 0.8 multiply_add_fusion.17
  40.3 0.8 multiply_add_fusion.16
  41.1 0.8 multiply_add_fusion.11
  41.9 0.7 multiply_add_fusion.10
  44.5 0.8 multiply_add_fusion.8
  46.0 0.8 multiply_add_fusion.4
  46.9 0.8 multiply_add_fusion.5
  49.0 1.1 copy.451
  50.2 1.1 copy.454
  51.3 1.1 copy.456
  52.6 1.1 copy.464
  53.7 1.1 copy.466
  62.4 0.9 copy-done.257
  68.5 0.7 copy-done.75
  70.9 13.4 %all-gather = f32[4,32,8]{1,2,0:T(8,128)S(1)} all-gather(f32[1,32,8]{1,2,0:T(8,128)S(1)} %multiply_bitcast_fusion), channel_id=1, replica_groups=mesh['gx'=2,'gy'=4,'gz'=4] {'gz'}, dimensions={0}, use_global_device_ids=true | all-gather | bytes 5120 | tf_op jit(solution)/shard_map/all_gather | solution.py:182
  85.0 0.7 copy-done.93
  85.8 0.7 copy-done.92
  86.6 0.7 copy-done.130
  87.3 0.7 copy-done.95
  97.0 1.9 collective-permute-start.2
  99.7 1.9 collective-permute-start.12
  101.6 3.0 %collective-permute-done.12 = f32[10,1]{1,0:T(8,128)S(1)} collective-permute-done((f32[10,1]{1,0:T(8,128)S(1)}, f32[10,1]{1,0:T(8,128)S(1)}, u32[]{:S(2)}, u32[]{:S(2)}) %collective-permute-start.12) | collective-permute-done | bytes 72 | tf_op jit(solution)/shard_map/ppermute | solution.py:25
  104.7 1.9 collective-permute-start.13
  106.6 1.3 collective-permute-done.13
  107.9 3.6 %collective-permute-start.3 = (f32[6,8,8,2]{3,2,1,0:T(8,128)S(1)}, f32[6,8,8,2]{3,2,1,0:T(8,128)S(1)}, u32[]{:S(2)}, u32[]{:S(2)}) collective-permute-start(f32[6,8,8,2]{3,2,1,0:T(8,128)S(1)} %get-tuple-element.208), channel_id=1, source_target_pairs={{4,0},{8,4},{12,8},{5,1},{9,5},{13,9},{6,2},{10,6},{14,10},{7,3},{... | collective-permute-start | bytes 9224 | tf_op jit(solution)/shard_map/ppermute | solution.py:26
  111.5 0.8 maximum_select_fusion.3
  112.3 15.1 %psum.7 = f32[10,130]{1,0:T(8,128)S(1)} all-reduce(f32[10,130]{1,0:T(8,128)S(1)} %maximum_select_fusion.3), channel_id=1, replica_groups=mesh['gx'=2,'gy'=4,'gz'=4] {'gz'}, use_global_device_ids=true, to_apply=%region_1.2 | all-reduce | flops 1300 | bytes 10400 | tf_op jit(solution)/shard_map/psum | solution.py:33
  127.5 0.8 fusion.159
  128.3 5.8 %collective-permute-start.1 = (f32[6,8,2,128]{3,2,1,0:T(2,128)}, f32[6,8,2,128]{3,2,1,0:T(2,128)}, u32[]{:S(2)}, u32[]{:S(2)}) collective-permute-start(f32[6,8,2,128]{3,2,1,0:T(2,128)} %get-tuple-element.210), channel_id=1, source_target_pairs={{16,0},{17,1},{18,2},{19,3},{20,4},{21,5},{22,6},{23,7},{24,8},{25... | collective-permute-start | bytes 147464 | tf_op jit(solution)/shard_map/ppermute | solution.py:26
  134.0 4.1 %collective-permute-start.4 = (f32[6,2,8,128]{3,2,1,0:T(8,128)}, f32[6,2,8,128]{3,2,1,0:T(8,128)}, u32[]{:S(2)}, u32[]{:S(2)}) collective-permute-start(f32[6,2,8,128]{3,2,1,0:T(8,128)} %get-tuple-element.205), channel_id=1, source_target_pairs={{0,1},{1,2},{2,3},{4,5},{5,6},{6,7},{8,9},{9,10},{10,11},{12,13},{... | collective-permute-start | bytes 147464 | tf_op jit(solution)/shard_map/ppermute | solution.py:25
  144.7 0.7 fusion.38
  145.6 0.8 slice_select_fusion.14
  146.5 0.8 slice_select_fusion.16
  147.4 0.7 slice_select_fusion.12
  149.4 0.9 pad_maximum_fusion
  150.6 1.0 copy.436
  151.6 2.6 %collective-permute-start.8 = (f32[3,16,20,2]{2,1,3,0:T(8,128)}, f32[3,16,20,2]{2,1,3,0:T(8,128)S(1)}, u32[]{:S(2)}, u32[]{:S(2)}) collective-permute-start(f32[3,16,20,2]{2,1,3,0:T(8,128)} %copy.436), channel_id=1, source_target_pairs={{0,1},{1,2},{2,3},{3,4},{4,5},{5,6},{6,7},{7,8},{8,9},{9,10},{10,1... | collective-permute-start | bytes 23048 | tf_op jit(solution)/shard_map/ppermute | solution.py:25
  154.6 3.2 %collective-permute-start.9 = (f32[3,16,20,2]{2,1,3,0:T(8,128)S(1)}, f32[3,16,20,2]{2,1,3,0:T(8,128)}, u32[]{:S(2)}, u32[]{:S(2)}) collective-permute-start(f32[3,16,20,2]{2,1,3,0:T(8,128)S(1)} %copy.437), channel_id=1, source_target_pairs={{1,0},{2,1},{3,2},{4,3},{5,4},{6,5},{7,6},{8,7},{9,8},{10,9},{11,1... | collective-permute-start | bytes 23048 | tf_op jit(solution)/shard_map/ppermute | solution.py:26
  160.2 6.3 %collective-permute-start.5 = (f32[6,2,8,128]{3,2,1,0:T(8,128)}, f32[6,2,8,128]{3,2,1,0:T(8,128)}, u32[]{:S(2)}, u32[]{:S(2)}) collective-permute-start(f32[6,2,8,128]{3,2,1,0:T(8,128)} %get-tuple-element.206), channel_id=1, source_target_pairs={{1,0},{2,1},{3,2},{5,4},{6,5},{7,6},{9,8},{10,9},{11,10},{13,12},{... | collective-permute-start | bytes 147464 | tf_op jit(solution)/shard_map/ppermute | solution.py:26
  166.9 1.2 copy.439
  168.1 1.0 maximum_bitcast_fusion
  169.6 0.7 copy-done.60
  171.3 1.5 slice_multiply_fusion.23
  172.8 1.1 slice_multiply_fusion.51
  173.9 0.8 pad_slice_fusion.5
  175.4 2.2 %fusion.4 = f32[1,16,16,64]{3,2,1,0:T(8,128)S(1)} fusion(f32[1,16,16,64]{3,2,1,0:T(8,128)S(1)} %get-tuple-element.104, f32[16,130]{1,0:T(8,128)S(1)} %copy-done.253, s32[64]{0:T(128)S(1)} %copy-done.264, s32[64]{0:T(128)S(1)} %copy-done.265, f32[16,16,64]{2,1,0:T(8,128)S(1)} %get-tuple-element.107, f32[16,16,64]{2,1,0:T(8,128)} %copy-done.258, ...), kind=kOutput, calls=%fused_computation.5 | convolution fusion | flops 1653376 | bytes 570380 | tf_op jit(solution)/shard_map/dot_general | solution.py:222
  190.4 0.8 copy-done.58
  193.3 1.0 copy.553
  194.2 1.0 copy.554
  195.2 0.9 maximum_maximum_fusion
  196.8 0.9 pad_maximum_fusion.2
  213.1 0.8 copy.551
  213.9 0.8 copy.552
  (811 shorter events, 85.2 us)
Async XLA Ops:
  2.3 147.1 %collective-permute-start.6 = (f32[3,16,2,64]{3,2,1,0:T(2,128)}, f32[3,16,2,64]{3,2,1,0:T(2,128)}, u32[]{:S(2)}, u32[]{:S(2)}) collective-permute-start(f32[3,16,2,64]{3,2,1,0:T(2,128)} %get-tuple-element.114), channel_id=1, source_target_pairs={{0,16},{1,17},{2,18},{3,19},{4,20},{5,21},{6,22},{7,23},{8,24},{9,... | collective-permute-start | bytes 73736 | tf_op jit(solution)/shard_map/ppermute | solution.py:25
  3.6 145.8 %collective-permute-start.7 = (f32[3,16,2,64]{3,2,1,0:T(2,128)}, f32[3,16,2,64]{3,2,1,0:T(2,128)}, u32[]{:S(2)}, u32[]{:S(2)}) collective-permute-start(f32[3,16,2,64]{3,2,1,0:T(2,128)} %get-tuple-element.115), channel_id=1, source_target_pairs={{16,0},{17,1},{18,2},{19,3},{20,4},{21,5},{22,6},{23,7},{24,8},{25... | collective-permute-start | bytes 73736 | tf_op jit(solution)/shard_map/ppermute | solution.py:26
  10.7 86.3 %collective-permute-start.10 = (f32[1,128]{1,0:T(1,128)}, f32[1,128]{1,0:T(1,128)}, u32[]{:S(2)}, u32[]{:S(2)}) collective-permute-start(f32[1,128]{1,0:T(1,128)} %get-tuple-element.134), channel_id=1, source_target_pairs={{0,16},{1,17},{2,18},{3,19},{4,20},{5,21},{6,22},{7,23},{8,24},{9,... | collective-permute-start | bytes 1544 | tf_op jit(solution)/shard_map/ppermute | solution.py:25
  11.9 7.4 %copy-start.1 = (f32[9,8,8,128]{3,2,1,0:T(8,128)S(1)}, f32[9,8,8,128]{3,2,1,0:T(8,128)}, u32[]{:S(2)}) copy-start(f32[9,8,8,128]{3,2,1,0:T(8,128)} %param.16) | copy-start | bytes 884740
  12.0 87.0 %collective-permute-start.11 = (f32[1,128]{1,0:T(1,128)}, f32[1,128]{1,0:T(1,128)}, u32[]{:S(2)}, u32[]{:S(2)}) collective-permute-start(f32[1,128]{1,0:T(1,128)} %get-tuple-element.135), channel_id=1, source_target_pairs={{16,0},{17,1},{18,2},{19,3},{20,4},{21,5},{22,6},{23,7},{24,8},{25... | collective-permute-start | bytes 1544 | tf_op jit(solution)/shard_map/ppermute | solution.py:26
  19.4 2.6 %copy-start = (f32[4,16,16,64]{3,2,1,0:T(8,128)S(1)}, f32[4,16,16,64]{3,2,1,0:T(8,128)}, u32[]{:S(2)}) copy-start(f32[4,16,16,64]{3,2,1,0:T(8,128)} %param.18) | copy-start | bytes 786436
  20.7 175.5 %collective-permute-start = (f32[6,8,2,128]{3,2,1,0:T(2,128)}, f32[6,8,2,128]{3,2,1,0:T(2,128)}, u32[]{:S(2)}, u32[]{:S(2)}) collective-permute-start(f32[6,8,2,128]{3,2,1,0:T(2,128)} %get-tuple-element.209), channel_id=1, source_target_pairs={{0,16},{1,17},{2,18},{3,19},{4,20},{5,21},{6,22},{7,23},{8,24},{9,... | collective-permute-start | bytes 147464 | tf_op jit(solution)/shard_map/ppermute | solution.py:25
  25.4 40.4 %copy-start.259 = (f32[16]{0:T(128)}, f32[16]{0:T(128)S(1)}, u32[]{:S(2)}) copy-start(f32[16]{0:T(128)S(1)} %get-tuple-element.498) | copy-start | bytes 196
  25.4 41.1 %copy-start.261 = (f32[16]{0:T(128)}, f32[16]{0:T(128)S(1)}, u32[]{:S(2)}) copy-start(f32[16]{0:T(128)S(1)} %get-tuple-element.499) | copy-start | bytes 196
  47.7 2.3 %copy-start.29 = (f32[16,16,1]{2,1,0:T(8,128)S(1)}, f32[16,16,1]{2,1,0:T(8,128)}, u32[]{:S(2)}) copy-start(f32[16,16,1]{2,1,0:T(8,128)} %get-tuple-element.245) | copy-start | bytes 3076
  50.2 2.2 %copy-start.28 = (f32[16,16,1]{2,1,0:T(8,128)S(1)}, f32[16,16,1]{2,1,0:T(8,128)}, u32[]{:S(2)}) copy-start(f32[16,16,1]{2,1,0:T(8,128)} %get-tuple-element.233) | copy-start | bytes 3076
  52.5 2.2 %copy-start.27 = (f32[16,16,1]{2,1,0:T(8,128)S(1)}, f32[16,16,1]{2,1,0:T(8,128)}, u32[]{:S(2)}) copy-start(f32[16,16,1]{2,1,0:T(8,128)} %get-tuple-element.243) | copy-start | bytes 3076
  65.2 2.7 %copy-start.258 = (f32[16,16,64]{2,1,0:T(8,128)}, f32[16,16,64]{2,1,0:T(8,128)S(1)}, u32[]{:S(2)}) copy-start(f32[16,16,64]{2,1,0:T(8,128)S(1)} %get-tuple-element.68) | copy-start | bytes 196612
  70.9 14.1 %copy-start.94 = (f32[8,8,1]{2,1,0:T(8,128)S(1)}, f32[8,8,1]{2,1,0:T(8,128)}, u32[]{:S(2)}) copy-start(f32[8,8,1]{2,1,0:T(8,128)} %get-tuple-element.420) | copy-start | bytes 772
  88.1 6.2 %copy-start.243 = (f32[8,1,128]{2,1,0:T(1,128)S(1)}, f32[8,1,128]{2,1,0:T(1,128)}, u32[]{:S(2)}) copy-start(f32[8,1,128]{2,1,0:T(1,128)} %get-tuple-element.360) | copy-start | bytes 12292
  88.1 6.2 %copy-start.244 = (f32[8,1,128]{2,1,0:T(1,128)S(1)}, f32[8,1,128]{2,1,0:T(1,128)}, u32[]{:S(2)}) copy-start(f32[8,1,128]{2,1,0:T(1,128)} %get-tuple-element.361) | copy-start | bytes 12292
  88.1 6.2 %copy-start.245 = (f32[8,1,128]{2,1,0:T(1,128)S(1)}, f32[8,1,128]{2,1,0:T(1,128)}, u32[]{:S(2)}) copy-start(f32[8,1,128]{2,1,0:T(1,128)} %get-tuple-element.364) | copy-start | bytes 12292
  88.1 6.2 %copy-start.246 = (f32[8,1,128]{2,1,0:T(1,128)S(1)}, f32[8,1,128]{2,1,0:T(1,128)}, u32[]{:S(2)}) copy-start(f32[8,1,128]{2,1,0:T(1,128)} %get-tuple-element.365) | copy-start | bytes 12292
  88.1 6.2 %copy-start.247 = (f32[8,1,128]{2,1,0:T(1,128)S(1)}, f32[8,1,128]{2,1,0:T(1,128)}, u32[]{:S(2)}) copy-start(f32[8,1,128]{2,1,0:T(1,128)} %get-tuple-element.367) | copy-start | bytes 12292
  88.1 6.2 %copy-start.248 = (f32[8,1,128]{2,1,0:T(1,128)S(1)}, f32[8,1,128]{2,1,0:T(1,128)}, u32[]{:S(2)}) copy-start(f32[8,1,128]{2,1,0:T(1,128)} %get-tuple-element.368) | copy-start | bytes 12292
  88.1 6.2 %copy-start.249 = (f32[8,1,128]{2,1,0:T(1,128)S(1)}, f32[8,1,128]{2,1,0:T(1,128)}, u32[]{:S(2)}) copy-start(f32[8,1,128]{2,1,0:T(1,128)} %get-tuple-element.369) | copy-start | bytes 12292
  88.1 4.7 %copy-start.250 = (f32[8,1,128]{2,1,0:T(1,128)S(1)}, f32[8,1,128]{2,1,0:T(1,128)}, u32[]{:S(2)}) copy-start(f32[8,1,128]{2,1,0:T(1,128)} %get-tuple-element.362) | copy-start | bytes 12292
  88.2 4.7 %copy-start.251 = (f32[8,1,128]{2,1,0:T(1,128)S(1)}, f32[8,1,128]{2,1,0:T(1,128)}, u32[]{:S(2)}) copy-start(f32[8,1,128]{2,1,0:T(1,128)} %get-tuple-element.366) | copy-start | bytes 12292
  88.2 5.4 %copy-start.226 = (f32[8,1,128]{2,1,0:T(1,128)S(1)}, f32[8,1,128]{2,1,0:T(1,128)}, u32[]{:S(2)}) copy-start(f32[8,1,128]{2,1,0:T(1,128)} %get-tuple-element.340) | copy-start | bytes 12292
  88.2 5.4 %copy-start.227 = (f32[8,1,128]{2,1,0:T(1,128)S(1)}, f32[8,1,128]{2,1,0:T(1,128)}, u32[]{:S(2)}) copy-start(f32[8,1,128]{2,1,0:T(1,128)} %get-tuple-element.399) | copy-start | bytes 12292
  88.9 2.2 %copy-start.194 = (f32[8,1,128]{2,1,0:T(1,128)S(1)}, f32[8,1,128]{2,1,0:T(1,128)}, u32[]{:S(2)}) copy-start(f32[8,1,128]{2,1,0:T(1,128)} %get-tuple-element.400) | copy-start | bytes 12292
  88.9 3.3 %copy-start.266 = (s32[16]{0:T(128)S(1)}, s32[16]{0:T(128)}, u32[]{:S(2)}) copy-start(s32[16]{0:T(128)} %param.20) | copy-start | bytes 196
  88.9 3.4 %copy-start.267 = (s32[64]{0:T(128)S(1)}, s32[64]{0:T(128)}, u32[]{:S(2)}) copy-start(s32[64]{0:T(128)} %param.21) | copy-start | bytes 772
  88.9 4.0 %copy-start.156 = (f32[8,1,128]{2,1,0:T(1,128)S(1)}, f32[8,1,128]{2,1,0:T(1,128)}, u32[]{:S(2)}) copy-start(f32[8,1,128]{2,1,0:T(1,128)} %get-tuple-element.371) | copy-start | bytes 12292
  89.0 4.5 %copy-start.106 = (f32[8,8,1]{2,1,0:T(8,128)S(1)}, f32[8,8,1]{2,1,0:T(8,128)}, u32[]{:S(2)}) copy-start(f32[8,8,1]{2,1,0:T(8,128)} %get-tuple-element.406) | copy-start | bytes 772
  89.0 4.5 %copy-start.107 = (f32[8,8,1]{2,1,0:T(8,128)S(1)}, f32[8,8,1]{2,1,0:T(8,128)}, u32[]{:S(2)}) copy-start(f32[8,8,1]{2,1,0:T(8,128)} %get-tuple-element.407) | copy-start | bytes 772
  89.0 4.5 %copy-start.108 = (f32[8,8,1]{2,1,0:T(8,128)S(1)}, f32[8,8,1]{2,1,0:T(8,128)}, u32[]{:S(2)}) copy-start(f32[8,8,1]{2,1,0:T(8,128)} %get-tuple-element.409) | copy-start | bytes 772
  89.0 4.6 %copy-start.192 = (f32[8,1,128]{2,1,0:T(1,128)S(1)}, f32[8,1,128]{2,1,0:T(1,128)}, u32[]{:S(2)}) copy-start(f32[8,1,128]{2,1,0:T(1,128)} %get-tuple-element.338) | copy-start | bytes 12292
  89.0 4.6 %copy-start.193 = (f32[8,1,128]{2,1,0:T(1,128)S(1)}, f32[8,1,128]{2,1,0:T(1,128)}, u32[]{:S(2)}) copy-start(f32[8,1,128]{2,1,0:T(1,128)} %get-tuple-element.397) | copy-start | bytes 12292
  89.0 5.9 %copy-start.74 = (f32[8,8,1]{2,1,0:T(8,128)S(1)}, f32[8,8,1]{2,1,0:T(8,128)}, u32[]{:S(2)}) copy-start(f32[8,8,1]{2,1,0:T(8,128)} %get-tuple-element.391) | copy-start | bytes 772
  90.4 3.2 %copy-start.59 = (f32[1,16,16,64]{3,2,1,0:T(8,128)}, f32[1,16,16,64]{3,2,1,0:T(8,128)S(1)}, u32[]{:S(2)}) copy-start(f32[1,16,16,64]{3,2,1,0:T(8,128)S(1)} %get-tuple-element.519) | copy-start | bytes 196612
  91.0 4.0 %copy-start.69 = (f32[8,8,1]{2,1,0:T(8,128)S(1)}, f32[8,8,1]{2,1,0:T(8,128)}, u32[]{:S(2)}) copy-start(f32[8,8,1]{2,1,0:T(8,128)} %get-tuple-element.386) | copy-start | bytes 772
  91.0 3.9 %copy-start.70 = (f32[8,8,1]{2,1,0:T(8,128)S(1)}, f32[8,8,1]{2,1,0:T(8,128)}, u32[]{:S(2)}) copy-start(f32[8,8,1]{2,1,0:T(8,128)} %get-tuple-element.387) | copy-start | bytes 772
  91.0 3.9 %copy-start.71 = (f32[8,8,1]{2,1,0:T(8,128)S(1)}, f32[8,8,1]{2,1,0:T(8,128)}, u32[]{:S(2)}) copy-start(f32[8,8,1]{2,1,0:T(8,128)} %get-tuple-element.388) | copy-start | bytes 772
  91.0 3.9 %copy-start.72 = (f32[8,8,1]{2,1,0:T(8,128)S(1)}, f32[8,8,1]{2,1,0:T(8,128)}, u32[]{:S(2)}) copy-start(f32[8,8,1]{2,1,0:T(8,128)} %get-tuple-element.389) | copy-start | bytes 772
  91.0 3.9 %copy-start.73 = (f32[8,8,1]{2,1,0:T(8,128)S(1)}, f32[8,8,1]{2,1,0:T(8,128)}, u32[]{:S(2)}) copy-start(f32[8,8,1]{2,1,0:T(8,128)} %get-tuple-element.390) | copy-start | bytes 772
  96.4 2.5 %copy-start.137 = (f32[8,128]{1,0:T(8,128)S(1)}, f32[8,128]{1,0:T(8,128)}, u32[]{:S(2)}) copy-start(f32[8,128]{1,0:T(8,128)} %get-tuple-element.136) | copy-start | bytes 12292
  97.0 31.3 %collective-permute-start.2 = (f32[6,8,8,2]{3,2,1,0:T(8,128)S(1)}, f32[6,8,8,2]{3,2,1,0:T(8,128)S(1)}, u32[]{:S(2)}, u32[]{:S(2)}) collective-permute-start(f32[6,8,8,2]{3,2,1,0:T(8,128)S(1)} %get-tuple-element.207), channel_id=1, source_target_pairs={{0,4},{4,8},{8,12},{1,5},{5,9},{9,13},{2,6},{6,10},{10,14},{3,7},{... | collective-permute-start | bytes 9224 | tf_op jit(solution)/shard_map/ppermute | solution.py:25
  99.7 5.0 %collective-permute-start.12 = (f32[10,1]{1,0:T(8,128)S(1)}, f32[10,1]{1,0:T(8,128)S(1)}, u32[]{:S(2)}, u32[]{:S(2)}) collective-permute-start(f32[10,1]{1,0:T(8,128)S(1)} %get-tuple-element.492), channel_id=1, source_target_pairs={{0,4},{4,8},{8,12},{1,5},{5,9},{9,13},{2,6},{6,10},{10,14},{3,7},{... | collective-permute-start | bytes 128 | tf_op jit(solution)/shard_map/ppermute | solution.py:25
  104.7 3.3 %collective-permute-start.13 = (f32[10,1]{1,0:T(8,128)S(1)}, f32[10,1]{1,0:T(8,128)S(1)}, u32[]{:S(2)}, u32[]{:S(2)}) collective-permute-start(f32[10,1]{1,0:T(8,128)S(1)} %get-tuple-element.493), channel_id=1, source_target_pairs={{4,0},{8,4},{12,8},{5,1},{9,5},{13,9},{6,2},{10,6},{14,10},{7,3},{... | collective-permute-start | bytes 128 | tf_op jit(solution)/shard_map/ppermute | solution.py:26
  107.9 26.1 %collective-permute-start.3 = (f32[6,8,8,2]{3,2,1,0:T(8,128)S(1)}, f32[6,8,8,2]{3,2,1,0:T(8,128)S(1)}, u32[]{:S(2)}, u32[]{:S(2)}) collective-permute-start(f32[6,8,8,2]{3,2,1,0:T(8,128)S(1)} %get-tuple-element.208), channel_id=1, source_target_pairs={{4,0},{8,4},{12,8},{5,1},{9,5},{13,9},{6,2},{10,6},{14,10},{7,3},{... | collective-permute-start | bytes 9224 | tf_op jit(solution)/shard_map/ppermute | solution.py:26
  127.4 10.7 %copy-start.34 = (f32[1,8,8,128]{3,2,1,0:T(8,128)S(1)}, f32[1,8,8,128]{3,2,1,0:T(8,128)}, u32[]{:S(2)}) copy-start(f32[1,8,8,128]{3,2,1,0:T(8,128)} %copy-done.33) | copy-start | bytes 98308
  127.4 10.7 %copy-start.36 = (f32[1,8,8,128]{3,2,1,0:T(8,128)S(1)}, f32[1,8,8,128]{3,2,1,0:T(8,128)}, u32[]{:S(2)}) copy-start(f32[1,8,8,128]{3,2,1,0:T(8,128)} %copy-done.35) | copy-start | bytes 98308
  128.3 67.9 %collective-permute-start.1 = (f32[6,8,2,128]{3,2,1,0:T(2,128)}, f32[6,8,2,128]{3,2,1,0:T(2,128)}, u32[]{:S(2)}, u32[]{:S(2)}) collective-permute-start(f32[6,8,2,128]{3,2,1,0:T(2,128)} %get-tuple-element.210), channel_id=1, source_target_pairs={{16,0},{17,1},{18,2},{19,3},{20,4},{21,5},{22,6},{23,7},{24,8},{25... | collective-permute-start | bytes 147464 | tf_op jit(solution)/shard_map/ppermute | solution.py:26
  134.0 61.2 %collective-permute-start.4 = (f32[6,2,8,128]{3,2,1,0:T(8,128)}, f32[6,2,8,128]{3,2,1,0:T(8,128)}, u32[]{:S(2)}, u32[]{:S(2)}) collective-permute-start(f32[6,2,8,128]{3,2,1,0:T(8,128)} %get-tuple-element.205), channel_id=1, source_target_pairs={{0,1},{1,2},{2,3},{4,5},{5,6},{6,7},{8,9},{9,10},{10,11},{12,13},{... | collective-permute-start | bytes 147464 | tf_op jit(solution)/shard_map/ppermute | solution.py:25
  151.6 8.5 %collective-permute-start.8 = (f32[3,16,20,2]{2,1,3,0:T(8,128)}, f32[3,16,20,2]{2,1,3,0:T(8,128)S(1)}, u32[]{:S(2)}, u32[]{:S(2)}) collective-permute-start(f32[3,16,20,2]{2,1,3,0:T(8,128)} %copy.436), channel_id=1, source_target_pairs={{0,1},{1,2},{2,3},{3,4},{4,5},{5,6},{6,7},{7,8},{8,9},{9,10},{10,1... | collective-permute-start | bytes 23048 | tf_op jit(solution)/shard_map/ppermute | solution.py:25
  154.6 12.3 %collective-permute-start.9 = (f32[3,16,20,2]{2,1,3,0:T(8,128)S(1)}, f32[3,16,20,2]{2,1,3,0:T(8,128)}, u32[]{:S(2)}, u32[]{:S(2)}) collective-permute-start(f32[3,16,20,2]{2,1,3,0:T(8,128)S(1)} %copy.437), channel_id=1, source_target_pairs={{1,0},{2,1},{3,2},{4,3},{5,4},{6,5},{7,6},{8,7},{9,8},{10,9},{11,1... | collective-permute-start | bytes 23048 | tf_op jit(solution)/shard_map/ppermute | solution.py:26
  160.1 9.5 %copy-start.52 = (f32[16,4,64]{2,1,0:T(4,128)}, f32[16,4,64]{2,1,0:T(4,128)S(1)}, u32[]{:S(2)}) copy-start(f32[16,4,64]{2,1,0:T(4,128)S(1)} %get-tuple-element.255) | copy-start | bytes 49156
  160.1 9.5 %copy-start.54 = (f32[16,4,64]{2,1,0:T(4,128)}, f32[16,4,64]{2,1,0:T(4,128)S(1)}, u32[]{:S(2)}) copy-start(f32[16,4,64]{2,1,0:T(4,128)S(1)} %get-tuple-element.256) | copy-start | bytes 49156
  160.2 35.0 %collective-permute-start.5 = (f32[6,2,8,128]{3,2,1,0:T(8,128)}, f32[6,2,8,128]{3,2,1,0:T(8,128)}, u32[]{:S(2)}, u32[]{:S(2)}) collective-permute-start(f32[6,2,8,128]{3,2,1,0:T(8,128)} %get-tuple-element.206), channel_id=1, source_target_pairs={{1,0},{2,1},{3,2},{5,4},{6,5},{7,6},{9,8},{10,9},{11,10},{13,12},{... | collective-permute-start | bytes 147464 | tf_op jit(solution)/shard_map/ppermute | solution.py:26
  197.9 1.9 copy-start.174
  201.5 2.4 %copy-start.158 = (f32[1,8,128]{2,1,0:T(8,128)S(1)}, f32[1,8,128]{2,1,0:T(8,128)}, u32[]{:S(2)}) copy-start(f32[1,8,128]{2,1,0:T(8,128)} %get-tuple-element.182) | copy-start | bytes 12292
  201.5 2.4 %copy-start.159 = (f32[1,8,128]{2,1,0:T(8,128)S(1)}, f32[1,8,128]{2,1,0:T(8,128)}, u32[]{:S(2)}) copy-start(f32[1,8,128]{2,1,0:T(8,128)} %get-tuple-element.183) | copy-start | bytes 12292
  201.5 2.4 %copy-start.160 = (f32[1,8,128]{2,1,0:T(8,128)S(1)}, f32[1,8,128]{2,1,0:T(8,128)}, u32[]{:S(2)}) copy-start(f32[1,8,128]{2,1,0:T(8,128)} %get-tuple-element.184) | copy-start | bytes 12292
  201.5 2.4 %copy-start.161 = (f32[1,8,128]{2,1,0:T(8,128)S(1)}, f32[1,8,128]{2,1,0:T(8,128)}, u32[]{:S(2)}) copy-start(f32[1,8,128]{2,1,0:T(8,128)} %get-tuple-element.185) | copy-start | bytes 12292
  201.5 2.4 %copy-start.239 = (f32[1,8,128]{2,1,0:T(8,128)S(1)}, f32[1,8,128]{2,1,0:T(8,128)}, u32[]{:S(2)}) copy-start(f32[1,8,128]{2,1,0:T(8,128)} %get-tuple-element.177) | copy-start | bytes 12292
  201.5 2.4 %copy-start.240 = (f32[1,8,128]{2,1,0:T(8,128)S(1)}, f32[1,8,128]{2,1,0:T(8,128)}, u32[]{:S(2)}) copy-start(f32[1,8,128]{2,1,0:T(8,128)} %get-tuple-element.178) | copy-start | bytes 12292
  201.5 2.4 %copy-start.241 = (f32[1,8,128]{2,1,0:T(8,128)S(1)}, f32[1,8,128]{2,1,0:T(8,128)}, u32[]{:S(2)}) copy-start(f32[1,8,128]{2,1,0:T(8,128)} %get-tuple-element.179) | copy-start | bytes 12292
  201.5 2.4 %copy-start.242 = (f32[1,8,128]{2,1,0:T(8,128)S(1)}, f32[1,8,128]{2,1,0:T(8,128)}, u32[]{:S(2)}) copy-start(f32[1,8,128]{2,1,0:T(8,128)} %get-tuple-element.180) | copy-start | bytes 12292
  (218 other events, 203.9 us)
where the time goes:
time: 218 us; the launch traced here: 215 us
  local copies, waits for them, and re-layouts  75.3 us (35%)
  other arithmetic  51.4 us (24%)
  starting transfers between devices  46.8 us (21%)
  blocking collectives  28.6 us (13%)
  between operations  5.11 us (2%)
  waiting for transfers between devices  4.42 us (2%)
  matrix products  3.04 us (1%)
    unnamed x556, local copies, waits for them, and re-layouts  41.2 us
    ppermute x7, starting transfers between devices, with_halo(): after = lax.ppermute(leading, axis, down)  32.4 us
    add x45, other arithmetic, closure(): running = running + weight * take_slab(field, col_index, 1, dimension)  25 us
    psum x1, blocking collectives, broadcast(): return lax.psum(block, axis)  15.1 us
    ppermute x7, starting transfers between devices, with_halo(): before = lax.ppermute(last, axis, up)  14.4 us
    all_gather x1, blocking collectives, body(): bed_pressure = lax.all_gather(bottom_part, 'gz', axis=1, tiled=True)  13.4 us
    mul x20, local copies, waits for them, and re-layouts, closure(): weight * take_slab(field, extent - 1 - col_index, 1, dimension)  6.82 us
    slice x7, local copies, waits for them, and re-layouts, with_halo(): last = lax.slice_in_dim(x, length - width, length, axis=dim)  5.06 us
  transfers between devices with their start and end apart: 14, of which 2 were waited for; matrix products, arithmetic and copies ran while one was open for 41% of the time, Pallas kernels for 0%

commit v1 on v0

v1 whole, which is shorter than its diff:
```python
import functools

import jax
import jax.numpy as jnp
from jax import lax
from jax.experimental import pallas as pl
from jax.experimental.pallas import tpu as pltpu
from jax.sharding import PartitionSpec as P

closure_rows = (
    (-24.0 / 17.0, 59.0 / 34.0, -4.0 / 17.0, -3.0 / 34.0, 0.0, 0.0),
    (-0.5, 0.0, 0.5, 0.0, 0.0, 0.0),
    (4.0 / 43.0, -59.0 / 86.0, 0.0, 59.0 / 86.0, -4.0 / 43.0, 0.0),
    (3.0 / 98.0, 0.0, -59.0 / 98.0, 0.0, 32.0 / 49.0, -4.0 / 49.0),
)
inv_norm = 48.0 / 17.0
step_size = 0.25
section_weight = 0.1496590219993
gravity = 0.4
interior_weights = {-2: 1.0 / 12.0, -1: -8.0 / 12.0, 1: 8.0 / 12.0, 2: -1.0 / 12.0}

x_fields = (0, 1, 2, 3, 8, 7)
y_fields = (0, 1, 2, 4, 8, 6)
z_fields = (0, 1, 2, 5, 6, 7)
ocean_x_fields = (1, 0)
ocean_y_fields = (2, 0)
rows, lanes, half = 8, 128, 64
far = 1 << 20


def turn(x, shift, axis):
    shift = shift % x.shape[axis]
    return x if shift == 0 else pltpu.roll(x, shift, axis)


def flag(value, shape=(rows, lanes)):
    return jnp.broadcast_to(value.astype(jnp.int32), shape) == 1


def lane_of(shape=(rows, lanes)):
    return lax.broadcasted_iota(jnp.int32, shape, 1)


def row_of(shape=(rows, lanes)):
    return lax.broadcasted_iota(jnp.int32, shape, 0)


def stencil(position, extent, first, last):
    low = position + far * (1 - first)
    high = extent - 1 - position + far * (1 - last)
    plain = jnp.logical_and(low >= 4, high >= 4)
    weights = {}
    for s in range(-3, 4):
        inside = jnp.logical_and(position + s >= 0, position + s < extent)
        w = jnp.where(jnp.logical_and(inside, plain), interior_weights.get(s, 0.0), 0.0)
        for r in range(4):
            if 0 <= r + s < 6 and closure_rows[r][r + s] != 0.0:
                w = jnp.where(low == r, closure_rows[r][r + s], w)
            if 0 <= r - s < 6 and closure_rows[r][r - s] != 0.0:
                w = jnp.where(high == r, -closure_rows[r][r - s], w)
        weights[s] = w
    return weights


def slope(x, weights, axis):
    total = weights[0] * x
    for s in (-3, -2, -1, 1, 2, 3):
        total = total + weights[s] * turn(x, -s, axis)
    return total


def pack_edges(tiles):
    group = lax.shift_right_logical(lane_of(), 2)
    out = []
    for start in range(0, len(tiles), 32):
        acc = jnp.zeros((rows, lanes), jnp.float32)
        for q, tile in enumerate(tiles[start : start + 32]):
            acc = jnp.where(group == q, turn(tile, 4 * q + 2, 1), acc)
        out.append(acc)
    return out


def edge_terms(left, right, has_left, has_right):
    place = jnp.bitwise_and(lane_of(), 3)
    low = jnp.where(
        place == 2, turn(left, 2, 1) - 8.0 * turn(left, 1, 1), turn(left, 2, 1)
    )
    high = jnp.where(
        place == 0, -turn(right, -2, 1), 8.0 * turn(right, -1, 1) - turn(right, -2, 1)
    )
    low = jnp.where(has_left, low, 0.0)
    high = jnp.where(has_right, high, 0.0)
    return jnp.where(place >= 2, low, high) * (1.0 / 12.0)


def row_terms(pack, from_low):
    even = jnp.bitwise_and(row_of(), 1) == 0
    low = jnp.where(even, pack - 8.0 * turn(pack, -1, 0), pack)
    high = jnp.where(even, -pack, 8.0 * turn(pack, 1, 0) - pack)
    return jnp.where(from_low, low, turn(high, 6, 0)) * (1.0 / 12.0)


def pair_rounds(size):
    first = [(i, i ^ 1) for i in range(size)]
    if size == 2:
        return (first,)
    second = [(i, (i + 1) % size if i % 2 else (i - 1) % size) for i in range(size)]
    return (first, second)


def where_am_i():
    return lax.axis_index("gx"), lax.axis_index("gy"), lax.axis_index("gz")


def paired_level(ocean, field, k, levels):
    a = ocean[field, k]
    b = ocean[field, k + levels // 2]
    return jnp.concatenate([a, b], axis=1)


def pack_x_kernel(solid, ocean, *outs):
    levels = ocean.shape[1]
    fine = ocean.shape[2]
    depth = solid.shape[1]
    odd = flag(lax.rem(lax.axis_index("gx"), 2))
    pair = lax.shift_right_logical(row_of(), 1)
    heads = []
    for field in x_fields:
        for z in range(depth):
            tile = solid[field, z]
            heads.append((tile, turn(tile, 2, 0)))
    for field in ocean_x_fields:
        for k in range(levels // 2):
            tile = paired_level(ocean, field, k, levels)
            heads.append((tile[:rows], turn(tile[fine - rows :], 2, 0)))
    for number, out in enumerate(outs):
        acc = None
        for t, (head, tail) in enumerate(heads):
            q = t % 4
            edge = jnp.where(odd, head, tail) if number == 0 else jnp.where(odd, tail, head)
            edge = turn(edge, 2 * q, 0)
            acc = edge if q == 0 else jnp.where(pair == q, edge, acc)
            if q == 3:
                out[t // 4] = acc


def row_rims(plane_packs, odd, single):
    if single:
        pack = plane_packs[0]
        return jnp.where(row_of() == 0, turn(pack, -1, 0), turn(pack, 1, 0))
    low = jnp.where(odd, plane_packs[0], plane_packs[1])
    high = jnp.where(odd, plane_packs[1], plane_packs[0])
    return jnp.where(row_of() == 0, turn(low, -1, 0), turn(high, 1, 0))


def pack_rest_kernel(count_x, solid, ocean, *refs):
    packs, (out_y, out_even, out_odd, out_bed, out_own) = refs[:count_x], refs[count_x:]
    levels, fine, width = ocean.shape[1:]
    depth = solid.shape[1]
    x, y, z = where_am_i()
    odd_x = flag(lax.rem(x, 2))
    odd_z = lax.rem(z, 2)
    plane_tile = (x_fields.index(2) * depth) // 4
    rim = row_rims([pack[plane_tile] for pack in packs], odd_x, count_x == 1)
    rim = jnp.where(row_of() < 2, rim, 0.0)
    tiles = [solid[field, k] for field in y_fields for k in range(depth)]
    packed = pack_edges(tiles)
    for i, tile in enumerate(packed):
        out_y[i] = tile
    out_y[len(packed)] = rim

    start_even = (1 - odd_z) * (depth - 2)
    start_odd = odd_z * (depth - 2)
    count = 0
    for field in z_fields:
        for k in range(2):
            out_even[count] = solid[field, start_even + k]
            out_odd[count] = solid[field, start_odd + k]
            count += 1
    outer, inner = [], []
    for field in ocean_y_fields:
        for k in range(levels // 2):
            tile = paired_level(ocean, field, k, levels)
            for r in range(0, fine, rows):
                outer.append(tile[r : r + rows])
                inner.append(turn(tile[r : r + rows], half, 1))
    for tile in pack_edges(outer) + pack_edges(inner):
        out_even[count] = tile
        out_odd[count] = tile
        count += 1

    deepest = ocean[0, levels - 1]
    pick_row = (
        lax.shift_right_logical(lax.broadcasted_iota(jnp.int32, (rows, fine), 1), 1)
        == lax.broadcasted_iota(jnp.int32, (rows, fine), 0)
    ).astype(jnp.float32)
    fine_col = lax.broadcasted_iota(jnp.int32, (width, lanes), 0)
    coarse_col = lax.broadcasted_iota(jnp.int32, (width, lanes), 1)
    pick_col = jnp.where(
        lax.shift_right_logical(fine_col, 1) + z * (width // 2) == coarse_col, 0.25, 0.0
    )
    dot = functools.partial(
        jnp.dot, precision=lax.Precision.HIGHEST, preferred_element_type=jnp.float32
    )
    pressure = dot(dot(pick_row, deepest), pick_col)
    bed = jnp.where(flag((z == 0)), solid[2, 0], pressure)
    for out in (out_even, out_odd):
        out[count] = bed
        out[count + 1] = rim
    out_bed[0] = bed
    out_bed[1] = rim
    out_own[0] = pressure
    out_own[1] = rim


def section_kernel(sizes, solid, material, ocean, medium, offset_x, offset_y, *refs):
    span_x, span_y, span_z = sizes
    count_x = len(pair_rounds(span_x))
    packs = refs[:count_x]
    got_y = refs[count_x : count_x + 2]
    got_ring = refs[count_x + 2 : count_x + 4]
    got_bed = refs[count_x + 4 : count_x + 4 + span_z - 2]
    solid_next, solid_rate, ocean_next, ocean_rate = refs[-5:-1]
    own_bed = refs[count_x + 4 + span_z - 2]
    row_scratch = refs[-1]
    levels, fine, width = ocean.shape[1:]
    depth = solid.shape[1]
    x, y, z = where_am_i()
    one = lambda condition: condition.astype(jnp.int32)
    x_first, x_last = one(x == 0), one(x == span_x - 1)
    y_first, y_last = one(y == 0), one(y == span_y - 1)
    z_first, z_last = one(z == 0), one(z == span_z - 1)
    odd_x, odd_y, odd_z = (flag(lax.rem(i, 2)) for i in (x, y, z))
    lane, row = lane_of(), row_of()

    def sides(got, odd, i):
        if len(got) == 1:
            return got[0][i], got[0][i]
        a, b = got[0][i], got[1][i]
        return jnp.where(odd, a, b), jnp.where(odd, b, a)

    has_low = flag(1 - x_first)
    has_high = flag(1 - x_last)
    pack_tiles = packs[0].shape[0]
    for i in range(pack_tiles):
        low, high = sides(packs, odd_x, i)
        if count_x == 1:
            row_scratch[0, i] = row_terms(low, odd_x)
        else:
            yes = jnp.full((rows, lanes), True)
            row_scratch[0, i] = row_terms(low, yes)
            row_scratch[1, i] = row_terms(high, jnp.logical_not(yes))
    low_rows = jnp.logical_and(row < 2, has_low)
    high_rows = jnp.logical_and(row >= rows - 2, has_high)
    end_rows = jnp.logical_or(low_rows, high_rows)

    def x_terms(t, mask_low, mask_high):
        q = t % 4
        if count_x == 1:
            tile = turn(row_scratch[0, t // 4], -2 * q, 0)
            return jnp.where(jnp.logical_or(mask_low, mask_high), tile, 0.0)
        low = turn(row_scratch[0, t // 4], -2 * q, 0)
        high = turn(row_scratch[1, t // 4], -2 * q, 0)
        return jnp.where(mask_low, low, jnp.where(mask_high, high, 0.0))

    edge_tiles = got_y[0].shape[0] - 1
    y_edges = []
    for i in range(edge_tiles):
        low, high = sides(got_y, odd_y, i)
        y_edges.append(edge_terms(low, high, flag(1 - y_first), flag(1 - y_last)))
    end_lanes = jnp.logical_or(lane < 2, lane >= lanes - 2)

    def y_terms(t):
        return jnp.where(end_lanes, turn(y_edges[t // 32], -(4 * (t % 32) + 2), 1), 0.0)

    weights_x = stencil(row, rows, x_first, x_last)
    weights_y = stencil(lane, lanes, y_first, y_last)
    at_first, at_last = flag(z_first), flag(z_last)
    ring_layers = 2 * len(z_fields)
    span_bed = ring_layers + 4

    def layer(i, k):
        if 0 <= k < depth:
            return solid[z_fields[i], k]
        low, high = sides(got_ring, odd_z, 2 * i + (k + 2 if k < 0 else k - depth))
        return low if k < 0 else high

    def slope_z(i, k):
        total = (
            layer(i, k - 2) - layer(i, k + 2) + 8.0 * (layer(i, k + 1) - layer(i, k - 1))
        ) * (1.0 / 12.0)
        if k < 4:
            near = sum(
                w * layer(i, c) for c, w in enumerate(closure_rows[k]) if w != 0.0
            )
            total = jnp.where(at_first, near, total)
        if depth - 1 - k < 4:
            near = sum(
                -w * layer(i, depth - 1 - c)
                for c, w in enumerate(closure_rows[depth - 1 - k])
                if w != 0.0
            )
            total = jnp.where(at_last, near, total)
        return total

    pressure = own_bed[0] + got_ring[0][span_bed - 2]
    for got in got_bed:
        pressure = pressure + got[0]

    for k in range(depth):
        dx = {
            m: slope(solid[m, k], weights_x, 0) + x_terms(i * depth + k, low_rows, high_rows)
            for i, m in enumerate(x_fields)
        }
        dy = {
            m: slope(solid[m, k], weights_y, 1) + y_terms(i * depth + k)
            for i, m in enumerate(y_fields)
        }
        metric = material[3, k]
        dz = {m: metric * slope_z(i, k) for i, m in enumerate(z_fields)}
        buoyancy, lame_one, lame_two = material[0, k], material[1, k], material[2, k]
        dilation = lame_one * (dx[0] + dy[1] + dz[2])
        twice = 2.0 * lame_two
        rates = [
            buoyancy * (dx[3] + dy[8] + dz[7]),
            buoyancy * (dx[8] + dy[4] + dz[6]),
            buoyancy * (dx[7] + dy[6] + dz[5]),
            dilation + twice * dx[0],
            dilation + twice * dy[1],
            dilation + twice * dz[2],
            lame_two * (dz[1] + dy[2]),
            lame_two * (dz[0] + dx[2]),
            lame_two * (dy[0] + dx[1]),
        ]
        if k == 0:
            factor = jnp.where(at_first, inv_norm * buoyancy * metric, 0.0)
            rates[0] = rates[0] + factor * solid[7, 0]
            rates[1] = rates[1] + factor * solid[6, 0]
            rates[2] = rates[2] + factor * (solid[5, 0] + pressure)
        for m, rate in enumerate(rates):
            rate = step_size * rate
            solid_rate[m, k] = rate
            solid_next[m, k] = solid[m, k] + section_weight * rate

    plane = solid[2, 0]
    rim_tile = own_bed[1]
    for d in range(1, span_z):
        got = got_ring[0] if d == 1 else got_bed[d - 2]
        offset = span_bed - 2 if d == 1 else 0
        here = flag(z == d)
        plane = jnp.where(here, got[offset], plane)
        rim_tile = jnp.where(here, got[offset + 1], rim_tile)
    t = y_fields.index(2) * depth
    left_edge, _ = sides(got_y, odd_y, t // 32)
    left_plane = turn(left_edge, lanes - 1 - (4 * (t % 32) + 1), 1)
    left_rim, _ = sides(got_y, odd_y, edge_tiles)
    _, right_plane = sides(got_ring, odd_z, span_bed - 2)
    _, right_rim = sides(got_ring, odd_z, span_bed - 1)
    beside_plane = jnp.where(lane == 0, right_plane, left_plane)
    beside_rim = jnp.where(lane == 0, right_rim, left_rim)
    dot = functools.partial(
        lax.dot_general,
        precision=lax.Precision.HIGHEST,
        preferred_element_type=jnp.float32,
    )
    fine_row = lax.broadcasted_iota(jnp.int32, (2 * rows, fine), 1)
    source_row = lax.broadcasted_iota(jnp.int32, (2 * rows, fine), 0)
    coarse = lax.shift_right_logical(fine_row, 1)
    low_end = -(x * rows)
    high_end = (span_x - x) * rows - 1
    target = jnp.clip(coarse + offset_x[...], low_end, high_end)
    target = jnp.where(target < 0, rows, jnp.where(target >= rows, rows + 1, target))
    blend_x = 0.75 * (source_row == coarse).astype(jnp.float32) + 0.25 * (
        source_row == target
    ).astype(jnp.float32)
    fine_col = lax.broadcasted_iota(jnp.int32, (lanes, lanes), 1)
    source_col = lax.broadcasted_iota(jnp.int32, (lanes, lanes), 0)
    coarse = lax.shift_right_logical(fine_col - half, 1) + z * (width // 2)
    shift_y = jnp.concatenate([offset_y[...], offset_y[...]], axis=1)
    target = jnp.clip(coarse + shift_y, -(y * lanes), (span_y - y) * lanes - 1)
    upper = fine_col >= half
    weight_near = jnp.where(upper, 0.75, 0.0)
    weight_far = jnp.where(upper, 0.25, 0.0)
    blend_y = jnp.where(source_col == coarse, weight_near, 0.0) + jnp.where(
        source_col == target, weight_far, 0.0
    )
    outside = jnp.logical_or(
        jnp.logical_and(source_col == lanes - 1, target == -1),
        jnp.logical_and(source_col == 0, target == lanes),
    )
    blend_beside = jnp.where(outside, weight_far, 0.0)
    contract_rows = (((0,), (0,)), ((), ()))
    plain = (((1,), (0,)), ((), ()))
    inside_rows = dot(blend_x, jnp.concatenate([plane, rim_tile], axis=0), contract_rows)
    beside_rows = dot(
        blend_x, jnp.concatenate([beside_plane, beside_rim], axis=0), contract_rows
    )
    bed_speed = dot(inside_rows, blend_y, plain) + dot(beside_rows, blend_beside, plain)

    pairs = levels // 2
    wide = (fine, lanes)
    lane2, row2 = lane_of(wide), row_of(wide)
    lower = lane2 < half
    joint_first, joint_last = y_first * z_first, y_last * z_last
    ocean_x = stencil(row2, fine, x_first, x_last)
    ocean_y = stencil(jnp.bitwise_and(lane2, half - 1), half, joint_first, joint_last)
    low_outer, high_outer = sides(got_ring, odd_z, ring_layers)
    low_inner, high_inner = sides(got_ring, odd_z, ring_layers + 1)
    has_left, has_right = flag(1 - joint_first), flag(1 - joint_last)
    outer = edge_terms(low_inner, high_inner, has_left, has_right)
    inner = edge_terms(low_outer, high_outer, has_left, has_right)
    mid_lanes = jnp.logical_and(lane >= half - 2, lane < half + 2)
    never = jnp.full((rows, lanes), False)

    def ocean_x_terms(t):
        low = x_terms(t, low_rows, never)
        high = x_terms(t, never, high_rows)
        middle = [jnp.zeros((fine - 2 * rows, lanes), jnp.float32)] if fine > 2 * rows else []
        return jnp.concatenate([low] + middle + [high], axis=0)

    def ocean_y_terms(t):
        parts = []
        for r in range(fine // rows):
            q = t * (fine // rows) + r
            end = turn(outer, -(4 * q + 2), 1)
            mid = turn(inner, half - (4 * q + 2), 1)
            parts.append(jnp.where(end_lanes, end, jnp.where(mid_lanes, mid, 0.0)))
        return jnp.concatenate(parts, axis=0)

    states = [[paired_level(ocean, m, k, levels) for k in range(pairs)] for m in range(4)]

    def ocean_z(m, k):
        def at(i):
            if 0 <= i < pairs:
                return states[m][i]
            return turn(states[m][i % pairs], half, 1)

        total = (at(k - 2) - at(k + 2) + 8.0 * (at(k + 1) - at(k - 1))) * (1.0 / 12.0)
        if k < 4:
            near = sum(w * at(c) for c, w in enumerate(closure_rows[k]) if w != 0.0)
            total = jnp.where(lower, near, total)
        if pairs - 1 - k < 4:
            near = sum(
                -w * at(pairs - 1 - c)
                for c, w in enumerate(closure_rows[pairs - 1 - k])
                if w != 0.0
            )
            total = jnp.where(lower, total, near)
        return total

    solid_packs = (len(x_fields) * depth) // 4 * 4
    for k in range(pairs):
        bulk = jnp.where(lower, medium[0, k], medium[0, k + pairs])
        light = jnp.where(lower, medium[1, k], medium[1, k + pairs])
        p, u, v, w = (states[m][k] for m in range(4))
        dxu = slope(u, ocean_x, 0) + ocean_x_terms(solid_packs + k)
        dxp = slope(p, ocean_x, 0) + ocean_x_terms(solid_packs + pairs + k)
        dyv = slope(v, ocean_y, 1) + ocean_y_terms(k)
        dyp = slope(p, ocean_y, 1) + ocean_y_terms(pairs + k)
        rate_p = -bulk * (2.0 * (dxu + dyv) + ocean_z(3, k)) + gravity * w / light
        rate_w = -light * ocean_z(0, k)
        if k == pairs - 1:
            rate_p = rate_p + jnp.where(lower, 0.0, inv_norm * bulk * (w - bed_speed))
        if k == 0:
            rate_w = rate_w - jnp.where(lower, inv_norm * light * p, 0.0)
        rates = (rate_p, -2.0 * light * dxp, -2.0 * light * dyp, rate_w)
        for m, rate in enumerate(rates):
            rate = step_size * rate
            after = states[m][k] + section_weight * rate
            ocean_rate[m, k] = rate[:, :half]
            ocean_next[m, k] = after[:, :half]
            ocean_rate[m, k + pairs] = turn(rate, half, 1)[:, :half]
            ocean_next[m, k + pairs] = turn(after, half, 1)[:, :half]


def body(solid_state, material, ocean_state, ocean_medium, offset_x, offset_y):
    sizes = tuple(lax.axis_size(axis) for axis in ("gx", "gy", "gz"))
    span_x, span_y, span_z = sizes
    depth = solid_state.shape[1]
    levels, fine, width = ocean_state.shape[1:]
    if solid_state.shape[2:] != (rows, lanes) or (fine, width) != (2 * rows, half):
        raise ValueError("tile shape")
    if depth % 4 or levels % 2 or span_z & (span_z - 1) or span_x % 2 or span_y % 2:
        raise ValueError("sizes")
    vmem = pl.BlockSpec(memory_space=pltpu.VMEM)
    smem = pl.BlockSpec(memory_space=pltpu.SMEM)
    f32 = jnp.float32
    tiles = lambda n: jax.ShapeDtypeStruct((n, rows, lanes), f32)
    x_rounds = pair_rounds(span_x)
    pack_tiles = (len(x_fields) * depth + len(ocean_x_fields) * levels // 2) // 4
    sent_x = pl.pallas_call(
        pack_x_kernel,
        out_shape=[tiles(pack_tiles) for _ in x_rounds],
        in_specs=[vmem, vmem],
        out_specs=[vmem for _ in x_rounds],
        name="pack_x",
    )(solid_state, ocean_state)
    got_x = [lax.ppermute(m, "gx", pairs) for m, pairs in zip(sent_x, x_rounds)]
    edge_tiles = -(-len(y_fields) * depth // 32)
    ring_tiles = 2 * len(z_fields) + 4
    sent_y, sent_even, sent_odd, sent_bed, own_bed = pl.pallas_call(
        functools.partial(pack_rest_kernel, len(got_x)),
        out_shape=[tiles(edge_tiles + 1), tiles(ring_tiles), tiles(ring_tiles), tiles(2), tiles(2)],
        in_specs=[vmem] * (2 + len(got_x)),
        out_specs=[vmem] * 5,
        name="pack_rest",
    )(solid_state, ocean_state, *got_x)
    y_rounds = pair_rounds(span_y)
    ring = ("gy", "gz")
    ring_rounds = pair_rounds(span_y * span_z)
    got_bed = [
        lax.ppermute(sent_bed, "gz", [(i, i ^ d) for i in range(span_z)])
        for d in range(2, span_z)
    ]
    got_ring = [
        lax.ppermute(m, ring, pairs) for m, pairs in zip((sent_even, sent_odd), ring_rounds)
    ]
    got_y = [lax.ppermute(sent_y, "gy", pairs) for pairs in y_rounds]
    if len(got_y) == 1:
        got_y = got_y * 2
    return pl.pallas_call(
        functools.partial(section_kernel, sizes),
        out_shape=[
            jax.ShapeDtypeStruct(solid_state.shape, f32),
            jax.ShapeDtypeStruct(solid_state.shape, f32),
            jax.ShapeDtypeStruct(ocean_state.shape, f32),
            jax.ShapeDtypeStruct(ocean_state.shape, f32),
        ],
        in_specs=[vmem, vmem, vmem, smem, vmem, vmem]
        + [vmem] * (len(got_x) + 4 + len(got_bed) + 1),
        out_specs=[vmem] * 4,
        scratch_shapes=[pltpu.VMEM((len(got_x), pack_tiles, rows, lanes), f32)],
        name="section",
    )(
        solid_state,
        material,
        ocean_state,
        ocean_medium,
        offset_x.reshape(1, fine),
        offset_y.reshape(1, width),
        *got_x,
        *got_y,
        *got_ring,
        *got_bed,
        own_bed,
    )


def solution(mesh):
    in_specs = (
        P(None, "gz", "gx", "gy"),
        P(None, "gz", "gx", "gy"),
        P(None, None, "gx", ("gy", "gz")),
        P(),
        P("gx"),
        P(("gy", "gz")),
    )
    out_specs = (
        P(None, "gz", "gx", "gy"),
        P(None, "gz", "gx", "gy"),
        P(None, None, "gx", ("gy", "gz")),
        P(None, None, "gx", ("gy", "gz")),
    )
    return jax.shard_map(body, mesh=mesh, in_specs=in_specs, out_specs=out_specs, check_vma=False)
```

time: 218 us -> 29.4 us (0.13)
  the two profiles are of different devices: /device:TPU:14 before, /device:TPU:0 now
where the time goes in v1:
time: 29.4 us; the launch traced here: 29.2 us
  starting transfers between devices  11.1 us (38%)
  waiting for transfers between devices  8.3 us (28%)
  Pallas kernels  7.83 us (27%)
  local copies, waits for them, and re-layouts  1.26 us (4%)
  between operations  0.69 us (2%)
    ppermute x2, waiting for transfers between devices, body(): lax.ppermute(sent_bed, 'gz', [(i, i ^ d) for i in range(span_z)])  5.83 us
    pallas_call x1, Pallas kernels, body(): pl.pallas_call(functools.partial(section_kernel, sizes), out_shape=[jax.S...  3.81 us
    ppermute x2, starting transfers between devices, body(): lax.ppermute(m, ring, pairs)  3.55 us
    ppermute x1, starting transfers between devices, body(): got_x = [lax.ppermute(m, 'gx', pairs) for m, pairs in zip(sent_x, x_rounds)]  2.97 us
    ppermute x1, waiting for transfers between devices, body(): got_x = [lax.ppermute(m, 'gx', pairs) for m, pairs in zip(sent_x, x_rounds)]  2.45 us
    ppermute x2, starting transfers between devices, body(): lax.ppermute(sent_bed, 'gz', [(i, i ^ d) for i in range(span_z)])  2.33 us
    ppermute x2, starting transfers between devices, body(): got_y = [lax.ppermute(sent_y, 'gy', pairs) for pairs in y_rounds]  2.25 us
    pallas_call x1, Pallas kernels, body(): pl.pallas_call(functools.partial(pack_rest_kernel, len(got_x)), out_shape...  2.15 us
  transfers between devices with their start and end apart: 7, of which 3 were waited for; matrix products, arithmetic and copies ran while one was open for 0% of the time, Pallas kernels for 0%

profile of v1, /device:TPU:0, one launch (start us, length us, event | category | flops | bytes accessed | tf_op | source)
XLA Modules:
  0.0 29.2 jit_solution(7004450550082393356)
XLA Ops:
  0.6 1.9 %pack_x.1 = f32[16,8,128]{2,1,0:T(8,128)} custom-call(f32[9,8,8,128]{3,2,1,0:T(8,128)} %solid.5, f32[4,16,16,64]{3,2,1,0:T(8,128)} %ocean.5), custom_call_target="tpu_custom_call" | custom-call | tf_op jit(solution)/shard_map/pack_x/pallas_call | solution.py:491
  2.5 3.0 %collective-permute-start = (f32[16,8,128]{2,1,0:T(8,128)}, f32[16,8,128]{2,1,0:T(8,128)S(1)}, u32[]{:S(2)}, u32[]{:S(2)}) collective-permute-start(f32[16,8,128]{2,1,0:T(8,128)} %pack_x.1), channel_id=1, source_target_pairs={{0,16},{16,0},{1,17},{17,1},{2,18},{18,2},{3,19},{19,3},{4,20},{20... | collective-permute-start | bytes 196616 | tf_op jit(solution)/shard_map/ppermute | solution.py:498
  5.5 2.5 %collective-permute-done.refs_0_ = f32[16,8,128]{2,1,0:T(8,128)S(1)} collective-permute-done((f32[16,8,128]{2,1,0:T(8,128)}, f32[16,8,128]{2,1,0:T(8,128)S(1)}, u32[]{:S(2)}, u32[]{:S(2)}) %collective-permute-start) | collective-permute-done | bytes 65568 | tf_op jit(solution)/shard_map/ppermute | solution.py:498
  7.9 0.0 copy-start
  7.9 0.6 %copy-done = f32[16,8,128]{2,1,0:T(8,128)} copy-done((f32[16,8,128]{2,1,0:T(8,128)}, f32[16,8,128]{2,1,0:T(8,128)S(1)}, u32[]{:S(2)}) %copy-start) | copy-done | bytes 65560
  8.5 2.1 %pack_rest.1 = (f32[3,8,128]{2,1,0:T(8,128)}, f32[16,8,128]{2,1,0:T(8,128)}, f32[16,8,128]{2,1,0:T(8,128)}, f32[2,8,128]{2,1,0:T(8,128)}, f32[2,8,128]{2,1,0:T(8,128)}) custom-call(f32[9,8,8,128]{3,2,1,0:T(8,128)} %solid.5, f32[4,16,16,64]{3,2,1,0:T(8,128)} %ocean.5, f32[16,8,128]{2,1,0:T(8,128)} %copy-done), custom_call_target="tpu_custom_call" | custom-call | tf_op jit(solution)/shard_map/pack_rest/pallas_call | solution.py:501
  10.7 2.1 %collective-permute-start.3 = (f32[16,8,128]{2,1,0:T(8,128)}, f32[16,8,128]{2,1,0:T(8,128)S(1)}, u32[]{:S(2)}, u32[]{:S(2)}) collective-permute-start(f32[16,8,128]{2,1,0:T(8,128)} %get-tuple-element.10), channel_id=1, source_target_pairs={{0,1},{1,0},{2,3},{3,2},{4,5},{5,4},{6,7},{7,6},{8,9},{9,8},{10,11... | collective-permute-start | bytes 196616 | tf_op jit(solution)/shard_map/ppermute | solution.py:516
  12.8 1.4 %collective-permute-start.4 = (f32[16,8,128]{2,1,0:T(8,128)}, f32[16,8,128]{2,1,0:T(8,128)S(1)}, u32[]{:S(2)}, u32[]{:S(2)}) collective-permute-start(f32[16,8,128]{2,1,0:T(8,128)} %get-tuple-element.11), channel_id=1, source_target_pairs={{0,15},{1,2},{2,1},{3,4},{4,3},{5,6},{6,5},{7,8},{8,7},{9,10},{10,... | collective-permute-start | bytes 196616 | tf_op jit(solution)/shard_map/ppermute | solution.py:516
  14.2 1.0 %collective-permute-start.6 = (f32[2,8,128]{2,1,0:T(8,128)}, f32[2,8,128]{2,1,0:T(8,128)S(1)}, u32[]{:S(2)}, u32[]{:S(2)}) collective-permute-start(f32[2,8,128]{2,1,0:T(8,128)} %get-tuple-element.12), channel_id=1, source_target_pairs={{0,3},{1,2},{2,1},{3,0},{4,7},{5,6},{6,5},{7,4},{8,11},{9,10},{10,... | collective-permute-start | bytes 24584 | tf_op jit(solution)/shard_map/ppermute | solution.py:512
  15.3 2.2 %collective-permute-start.2 = (f32[3,8,128]{2,1,0:T(8,128)}, f32[3,8,128]{2,1,0:T(8,128)S(1)}, u32[]{:S(2)}, u32[]{:S(2)}) collective-permute-start(f32[3,8,128]{2,1,0:T(8,128)} %get-tuple-element.9), channel_id=1, source_target_pairs={{0,12},{4,8},{8,4},{12,0},{1,13},{5,9},{9,5},{13,1},{2,14},{6,10},... | collective-permute-start | bytes 36872 | tf_op jit(solution)/shard_map/ppermute | solution.py:518
  17.5 0.0 collective-permute-start.1
  17.5 2.4 %collective-permute-done.6.refs_6_ = f32[2,8,128]{2,1,0:T(8,128)S(1)} collective-permute-done((f32[2,8,128]{2,1,0:T(8,128)}, f32[2,8,128]{2,1,0:T(8,128)S(1)}, u32[]{:S(2)}, u32[]{:S(2)}) %collective-permute-start.6) | collective-permute-done | bytes 8224 | tf_op jit(solution)/shard_map/ppermute | solution.py:512
  19.9 0.0 copy-start.5
  19.9 1.3 %collective-permute-start.5 = (f32[2,8,128]{2,1,0:T(8,128)}, f32[2,8,128]{2,1,0:T(8,128)S(1)}, u32[]{:S(2)}, u32[]{:S(2)}) collective-permute-start(f32[2,8,128]{2,1,0:T(8,128)} %get-tuple-element.12), channel_id=1, source_target_pairs={{0,2},{1,3},{2,0},{3,1},{4,6},{5,7},{6,4},{7,5},{8,10},{9,11},{10,... | collective-permute-start | bytes 24584 | tf_op jit(solution)/shard_map/ppermute | solution.py:512
  21.2 3.5 %collective-permute-done.5.refs_5_ = f32[2,8,128]{2,1,0:T(8,128)S(1)} collective-permute-done((f32[2,8,128]{2,1,0:T(8,128)}, f32[2,8,128]{2,1,0:T(8,128)S(1)}, u32[]{:S(2)}, u32[]{:S(2)}) %collective-permute-start.5) | collective-permute-done | bytes 8224 | tf_op jit(solution)/shard_map/ppermute | solution.py:512
  24.7 0.0 copy-start.6
  24.7 0.0 collective-permute-done.2.refs_2_
  24.7 0.0 copy-start.3
  24.7 0.0 collective-permute-done.1.refs_1_
  24.7 0.0 copy-start.4
  24.7 0.0 collective-permute-done.3.refs_3_
  24.7 0.0 copy-start.1
  24.7 0.0 collective-permute-done.4.refs_4_
  24.7 0.0 copy-start.2
  24.7 0.0 copy-done.5
  24.7 0.5 %copy-done.6 = f32[2,8,128]{2,1,0:T(8,128)} copy-done((f32[2,8,128]{2,1,0:T(8,128)}, f32[2,8,128]{2,1,0:T(8,128)S(1)}, u32[]{:S(2)}) %copy-start.6) | copy-done | bytes 8216
  25.3 0.0 copy-done.3
  25.3 0.0 copy-done.4
  25.3 0.1 copy-done.1
  25.3 0.0 copy-done.2
  25.4 3.8 %section.1 = (f32[9,8,8,128]{3,2,1,0:T(8,128)}, f32[9,8,8,128]{3,2,1,0:T(8,128)}, f32[4,16,16,64]{3,2,1,0:T(8,128)}, f32[4,16,16,64]{3,2,1,0:T(8,128)}) custom-call(f32[9,8,8,128]{3,2,1,0:T(8,128)} %solid.5, f32[4,8,8,128]{3,2,1,0:T(8,128)} %material.1, f32[4,16,16,64]{3,2,1,0:T(8,128)} %ocean.5, f32[2,16]{1,0:T(2,128)} %medium.1, s32[1,16]{1,0:T(1,128)} %bitcast.2, ...), custom_call_target="tpu_custom_call" | custom-call | tf_op jit(solution)/shard_map/section/pallas_call | solution.py:521
Async XLA Ops:
  2.5 5.4 %collective-permute-start = (f32[16,8,128]{2,1,0:T(8,128)}, f32[16,8,128]{2,1,0:T(8,128)S(1)}, u32[]{:S(2)}, u32[]{:S(2)}) collective-permute-start(f32[16,8,128]{2,1,0:T(8,128)} %pack_x.1), channel_id=1, source_target_pairs={{0,16},{16,0},{1,17},{17,1},{2,18},{18,2},{3,19},{19,3},{4,20},{20... | collective-permute-start | bytes 196616 | tf_op jit(solution)/shard_map/ppermute | solution.py:498
  7.9 0.6 %copy-start = (f32[16,8,128]{2,1,0:T(8,128)}, f32[16,8,128]{2,1,0:T(8,128)S(1)}, u32[]{:S(2)}) copy-start(f32[16,8,128]{2,1,0:T(8,128)S(1)} %collective-permute-done.refs_0_) | copy-start | bytes 196612
  10.7 14.0 %collective-permute-start.3 = (f32[16,8,128]{2,1,0:T(8,128)}, f32[16,8,128]{2,1,0:T(8,128)S(1)}, u32[]{:S(2)}, u32[]{:S(2)}) collective-permute-start(f32[16,8,128]{2,1,0:T(8,128)} %get-tuple-element.10), channel_id=1, source_target_pairs={{0,1},{1,0},{2,3},{3,2},{4,5},{5,4},{6,7},{7,6},{8,9},{9,8},{10,11... | collective-permute-start | bytes 196616 | tf_op jit(solution)/shard_map/ppermute | solution.py:516
  12.8 11.9 %collective-permute-start.4 = (f32[16,8,128]{2,1,0:T(8,128)}, f32[16,8,128]{2,1,0:T(8,128)S(1)}, u32[]{:S(2)}, u32[]{:S(2)}) collective-permute-start(f32[16,8,128]{2,1,0:T(8,128)} %get-tuple-element.11), channel_id=1, source_target_pairs={{0,15},{1,2},{2,1},{3,4},{4,3},{5,6},{6,5},{7,8},{8,7},{9,10},{10,... | collective-permute-start | bytes 196616 | tf_op jit(solution)/shard_map/ppermute | solution.py:516
  14.2 5.7 %collective-permute-start.6 = (f32[2,8,128]{2,1,0:T(8,128)}, f32[2,8,128]{2,1,0:T(8,128)S(1)}, u32[]{:S(2)}, u32[]{:S(2)}) collective-permute-start(f32[2,8,128]{2,1,0:T(8,128)} %get-tuple-element.12), channel_id=1, source_target_pairs={{0,3},{1,2},{2,1},{3,0},{4,7},{5,6},{6,5},{7,4},{8,11},{9,10},{10,... | collective-permute-start | bytes 24584 | tf_op jit(solution)/shard_map/ppermute | solution.py:512
  15.3 9.4 %collective-permute-start.2 = (f32[3,8,128]{2,1,0:T(8,128)}, f32[3,8,128]{2,1,0:T(8,128)S(1)}, u32[]{:S(2)}, u32[]{:S(2)}) collective-permute-start(f32[3,8,128]{2,1,0:T(8,128)} %get-tuple-element.9), channel_id=1, source_target_pairs={{0,12},{4,8},{8,4},{12,0},{1,13},{5,9},{9,5},{13,1},{2,14},{6,10},... | collective-permute-start | bytes 36872 | tf_op jit(solution)/shard_map/ppermute | solution.py:518
  17.5 7.1 %collective-permute-start.1 = (f32[3,8,128]{2,1,0:T(8,128)}, f32[3,8,128]{2,1,0:T(8,128)S(1)}, u32[]{:S(2)}, u32[]{:S(2)}) collective-permute-start(f32[3,8,128]{2,1,0:T(8,128)} %get-tuple-element.9), channel_id=1, source_target_pairs={{0,4},{4,0},{8,12},{12,8},{1,5},{5,1},{9,13},{13,9},{2,6},{6,2},{1... | collective-permute-start | bytes 36872 | tf_op jit(solution)/shard_map/ppermute | solution.py:518
  19.9 4.8 %copy-start.5 = (f32[2,8,128]{2,1,0:T(8,128)}, f32[2,8,128]{2,1,0:T(8,128)S(1)}, u32[]{:S(2)}) copy-start(f32[2,8,128]{2,1,0:T(8,128)S(1)} %collective-permute-done.6.refs_6_) | copy-start | bytes 24580
  19.9 4.8 %collective-permute-start.5 = (f32[2,8,128]{2,1,0:T(8,128)}, f32[2,8,128]{2,1,0:T(8,128)S(1)}, u32[]{:S(2)}, u32[]{:S(2)}) collective-permute-start(f32[2,8,128]{2,1,0:T(8,128)} %get-tuple-element.12), channel_id=1, source_target_pairs={{0,2},{1,3},{2,0},{3,1},{4,6},{5,7},{6,4},{7,5},{8,10},{9,11},{10,... | collective-permute-start | bytes 24584 | tf_op jit(solution)/shard_map/ppermute | solution.py:512
  24.7 0.6 %copy-start.6 = (f32[2,8,128]{2,1,0:T(8,128)}, f32[2,8,128]{2,1,0:T(8,128)S(1)}, u32[]{:S(2)}) copy-start(f32[2,8,128]{2,1,0:T(8,128)S(1)} %collective-permute-done.5.refs_5_) | copy-start | bytes 24580
  24.7 0.6 %copy-start.3 = (f32[3,8,128]{2,1,0:T(8,128)}, f32[3,8,128]{2,1,0:T(8,128)S(1)}, u32[]{:S(2)}) copy-start(f32[3,8,128]{2,1,0:T(8,128)S(1)} %collective-permute-done.2.refs_2_) | copy-start | bytes 36868
  24.7 0.6 %copy-start.4 = (f32[3,8,128]{2,1,0:T(8,128)}, f32[3,8,128]{2,1,0:T(8,128)S(1)}, u32[]{:S(2)}) copy-start(f32[3,8,128]{2,1,0:T(8,128)S(1)} %collective-permute-done.1.refs_1_) | copy-start | bytes 36868
  24.7 0.6 %copy-start.1 = (f32[16,8,128]{2,1,0:T(8,128)}, f32[16,8,128]{2,1,0:T(8,128)S(1)}, u32[]{:S(2)}) copy-start(f32[16,8,128]{2,1,0:T(8,128)S(1)} %collective-permute-done.3.refs_3_) | copy-start | bytes 196612
  24.7 0.7 %copy-start.2 = (f32[16,8,128]{2,1,0:T(8,128)}, f32[16,8,128]{2,1,0:T(8,128)S(1)}, u32[]{:S(2)}) copy-start(f32[16,8,128]{2,1,0:T(8,128)S(1)} %collective-permute-done.4.refs_4_) | copy-start | bytes 196612
